TPU v7x, 32 devices: a whole 2x2x4 slice. The times are simulated.
32 devices in a mesh: fsdp: 4 (over y, core), ctx: 2 (over x), tp: 4 (over z).
Axes of the slice: x: 2, y: 2, z: 4, core: 2. Of those that a mesh axis runs over, the one named last changes fastest.
Arguments:
- tokens: bfloat16 [4, 1024, 2048], P('fsdp', 'ctx'), may hold values from -6 to 6
- lengths: int32 [4, 3], P('fsdp'), may hold values from 1 to 768, 960 in all within a row
- block_order: int32 [4, 4], P('fsdp'), may hold values from 0 to 3, each once within a row
- ln_gain: bfloat16 [2048], P('fsdp'), may hold values from 0.25 to 1.75
- ln_bias: bfloat16 [2048], P('fsdp'), may hold values from -3 to 3
- qkv_weight: bfloat16 [2048, 3, 2048], P('fsdp', None, 'tp'), may hold values from -0.125 to 0.125
- qkv_bias: bfloat16 [3, 2048], P(None, 'tp'), may hold values from -0.59765625 to 0.59765625
- dense_weight: bfloat16 [2048, 2048], P('fsdp', 'tp'), may hold values from -1 to 1
- dense_bias: bfloat16 [2048], P('fsdp'), may hold values from -3 to 3
- fc1_weight: bfloat16 [2048, 8192], P('fsdp', 'tp'), may hold values from -0.125 to 0.125
- fc1_bias: bfloat16 [8192], P('tp'), may hold values from -3 to 3
- fc2_weight: bfloat16 [2048, 8192], P('fsdp', 'tp'), may hold values from -0.0625 to 0.0625
- fc2_bias: bfloat16 [2048], P('fsdp'), may hold values from -3 to 3
- cotangent: bfloat16 [4, 1024, 2048], P('fsdp', 'ctx'), may hold values from -6 to 6
Outputs:
- output: bfloat16 [4, 1024, 2048], P('fsdp', 'ctx')
- input_grad: float32 [4, 1024, 2048], P('fsdp', 'ctx')
- ln_gain_grad: float32 [2048], P('fsdp')
- ln_bias_grad: float32 [2048], P('fsdp')
- qkv_weight_grad: float32 [2048, 3, 2048], P('fsdp', None, 'tp')
- qkv_bias_grad: float32 [3, 2048], P(None, 'tp')
- dense_weight_grad: float32 [2048, 2048], P('fsdp', 'tp')
- dense_bias_grad: float32 [2048], P('fsdp')
- fc1_weight_grad: float32 [2048, 8192], P('fsdp', 'tp')
- fc1_bias_grad: float32 [8192], P('tp')
- fc2_weight_grad: float32 [2048, 8192], P('fsdp', 'tp')
- fc2_bias_grad: float32 [2048], P('fsdp')
Inputs may be any that keep to these rules, and one draw needn't show every extreme that they name: Each row holds the lengths of 3 sequences packed from the row's start; they sum to 960 and the largest is exactly 768. Each row is a permutation of the 4 block numbers; dealt block j holds packed block block_order[b, j].
All inputs are finite; a program needn't handle non-finite values.
Results may differ from a plain program's by a relative error of at most 0.012.
Values may be sent and summed in bfloat16 or wider, within the bound.
No kernel may reach another device: no remote copies, remote signals or barrier semaphores. Data moves between devices by JAX's collectives and lax.ppermute only.
A program may use at most 256 MiB of HBM per device.

v0:
```python
import math
import jax
import jax.numpy as jnp
from jax import lax
from jax.sharding import PartitionSpec as P

HD = 256
ROT = 64
NORM_EPSILON = 1e-05
MASK_FLOOR = -1000000000.0


def rotation_tables(position):
    frequency = jnp.exp(jnp.arange(ROT // 2, dtype=jnp.float32) * (-2.0 * math.log(10000.0) / ROT))
    angles = position.astype(jnp.float32)[:, None] * frequency[None, :]
    return (jnp.cos(angles)[:, None, :], jnp.sin(angles)[:, None, :])


def rotate(values, cosine_table, sine_table):
    first_half = values[..., : ROT // 2]
    second_half = values[..., ROT // 2 : ROT]
    return jnp.concatenate(
        [
            first_half * cosine_table - second_half * sine_table,
            second_half * cosine_table + first_half * sine_table,
            values[..., ROT:],
        ],
        axis=-1,
    )


def rotate_back(grads, cosine_table, sine_table):
    first_half = grads[..., : ROT // 2]
    second_half = grads[..., ROT // 2 : ROT]
    return jnp.concatenate(
        [
            first_half * cosine_table + second_half * sine_table,
            second_half * cosine_table - first_half * sine_table,
            grads[..., ROT:],
        ],
        axis=-1,
    )


def packed_rows(order_row, first_slot, row_count, block_rows):
    row_index = jnp.arange(row_count, dtype=jnp.int32)
    dealt_slot = first_slot + row_index // block_rows
    selector = dealt_slot[:, None] == jnp.arange(order_row.shape[0], dtype=jnp.int32)[None, :]
    source_block = jnp.sum(jnp.where(selector, order_row[None, :], 0), axis=1, dtype=jnp.int32)
    return source_block * block_rows + row_index % block_rows


def place_rows(packed_at, lengths_row):
    seq_ends = jnp.cumsum(lengths_row, dtype=jnp.int32)
    passed = packed_at[:, None] >= seq_ends[None, :]
    segment = jnp.sum(passed.astype(jnp.int32), axis=1, dtype=jnp.int32)
    before = jnp.sum(jnp.where(passed, lengths_row[None, :], 0), axis=1, dtype=jnp.int32)
    return (segment, packed_at - before)


def gelu_slope(value):
    normal_cdf = 0.5 * (1.0 + lax.erf(value * (1.0 / math.sqrt(2.0))))
    density = jnp.exp(-0.5 * value * value) * (1.0 / math.sqrt(2.0 * math.pi))
    return normal_cdf + value * density


def per_device(
    tokens,
    lengths,
    block_order,
    ln_gain,
    ln_bias,
    qkv_weight,
    qkv_bias,
    dense_weight,
    dense_bias,
    fc1_weight,
    fc1_bias,
    fc2_weight,
    fc2_bias,
    cotangent,
):
    gathered = (
        lax.all_gather(qkv_weight, "fsdp", axis=0, tiled=True),
        lax.all_gather(dense_weight, "fsdp", axis=0, tiled=True),
        lax.all_gather(fc1_weight, "fsdp", axis=0, tiled=True),
        lax.all_gather(fc2_weight, "fsdp", axis=0, tiled=True),
        lax.all_gather(ln_gain, "fsdp", axis=0, tiled=True),
        lax.all_gather(ln_bias, "fsdp", axis=0, tiled=True),
        lax.all_gather(dense_bias, "fsdp", axis=0, tiled=True),
        lax.all_gather(fc2_bias, "fsdp", axis=0, tiled=True),
    )
    qkv_full = gathered[0]
    dense_full = gathered[1]
    fc1_full = gathered[2]
    fc2_full = gathered[3]
    norm_gain = gathered[4].astype(jnp.float32)
    norm_bias = gathered[5].astype(jnp.float32)
    out_bias = gathered[6].astype(jnp.float32) + gathered[7].astype(jnp.float32)
    inputs = tokens[0].astype(jnp.float32)
    row_count = inputs.shape[0]
    block_rows = row_count // 2
    group_rows = row_count * lax.axis_size("ctx")
    lengths_row = lengths[0]
    order_row = block_order[0]
    seq_count = lengths_row.shape[0]
    local_packed = packed_rows(order_row, lax.axis_index("ctx") * 2, row_count, block_rows)
    key_packed = packed_rows(order_row, 0, group_rows, block_rows)
    local_segment, local_position = place_rows(local_packed, lengths_row)
    key_segment = place_rows(key_packed, lengths_row)[0]
    valid_rows = (local_segment < seq_count).astype(jnp.float32)
    allowed = (local_segment[:, None] == key_segment[None, :]) & (
        key_packed[None, :] <= local_packed[:, None]
    )
    cosine_table, sine_table = rotation_tables(local_position)
    score_scale = 1.0 / math.sqrt(HD)
    row_mean = jnp.mean(inputs, axis=1, keepdims=True)
    centred = inputs - row_mean
    variance = jnp.mean(centred * centred, axis=1, keepdims=True)
    inverse = lax.rsqrt(variance + NORM_EPSILON)
    standard = centred * inverse
    normed = (standard * norm_gain + norm_bias).astype(jnp.bfloat16)
    projected = jnp.einsum(
        "td,dce->tce", normed, qkv_full, preferred_element_type=jnp.float32
    ) + qkv_bias.astype(jnp.float32)
    heads_here = projected.shape[2] // HD
    shaped = projected.reshape(row_count, 3, heads_here, HD)
    queries = rotate(shaped[:, 0], cosine_table, sine_table).astype(jnp.bfloat16)
    keys_local = rotate(shaped[:, 1], cosine_table, sine_table).astype(jnp.bfloat16)
    values_local = shaped[:, 2].astype(jnp.bfloat16)
    keys_all, values_all = (
        lax.all_gather(keys_local, "ctx", axis=0, tiled=True),
        lax.all_gather(values_local, "ctx", axis=0, tiled=True),
    )

    def head_scores(head_index):
        scores = (
            jnp.einsum(
                "qe,ke->qk",
                queries[:, head_index],
                keys_all[:, head_index],
                preferred_element_type=jnp.float32,
            )
            * score_scale
        )
        return jnp.where(allowed, scores, MASK_FLOOR)

    head_outputs = []
    log_totals = []
    for head_index in range(heads_here):
        scores = head_scores(head_index)
        row_max = jnp.max(scores, axis=1, keepdims=True)
        exp_scores = jnp.exp(scores - row_max)
        row_total = jnp.sum(exp_scores, axis=1, keepdims=True)
        probabilities = (exp_scores / row_total).astype(jnp.bfloat16)
        head_outputs.append(
            jnp.dot(probabilities, values_all[:, head_index], preferred_element_type=jnp.float32)
        )
        log_totals.append(row_max + jnp.log(row_total))
    attended = (
        (jnp.stack(head_outputs, axis=1) * valid_rows[:, None, None])
        .astype(jnp.bfloat16)
        .reshape(row_count, heads_here * HD)
    )
    pre_act = jnp.dot(normed, fc1_full, preferred_element_type=jnp.float32) + fc1_bias.astype(
        jnp.float32
    )
    hidden = jax.nn.gelu(pre_act, approximate=False).astype(jnp.bfloat16)
    partial_out = jnp.einsum(
        "te,de->td", attended, dense_full, preferred_element_type=jnp.float32
    ) + jnp.einsum("tf,df->td", hidden, fc2_full, preferred_element_type=jnp.float32)
    summed = lax.psum(partial_out, "tp")
    output = (inputs + summed + out_bias).astype(jnp.bfloat16)
    upstream_low = cotangent[0]
    upstream = upstream_low.astype(jnp.float32)
    out_bias_grad = jnp.sum(upstream, axis=0)
    dense_grad = jnp.einsum("td,te->de", upstream_low, attended, preferred_element_type=jnp.float32)
    fc2_grad = jnp.einsum("td,tf->df", upstream_low, hidden, preferred_element_type=jnp.float32)
    attended_grad = (
        jnp.dot(upstream_low, dense_full, preferred_element_type=jnp.float32).astype(jnp.bfloat16)
        * valid_rows[:, None].astype(jnp.bfloat16)
    ).reshape(row_count, heads_here, HD)
    hidden_grad = jnp.dot(upstream_low, fc2_full, preferred_element_type=jnp.float32)
    pre_grad = (hidden_grad * gelu_slope(pre_act)).astype(jnp.bfloat16)
    fc1_bias_grad = jnp.sum(pre_grad.astype(jnp.float32), axis=0)
    fc1_grad = jnp.einsum("td,tf->df", normed, pre_grad, preferred_element_type=jnp.float32)
    normed_grad = jnp.einsum("tf,df->td", pre_grad, fc1_full, preferred_element_type=jnp.float32)
    query_pieces = []
    key_pieces = []
    value_pieces = []
    for head_index in range(heads_here):
        probs_full = jnp.exp(head_scores(head_index) - log_totals[head_index])
        probs_low = probs_full.astype(jnp.bfloat16)
        head_grad = attended_grad[:, head_index]
        prob_grad = jnp.einsum(
            "qe,ke->qk", head_grad, values_all[:, head_index], preferred_element_type=jnp.float32
        )
        row_delta = jnp.sum(probs_full * prob_grad, axis=1, keepdims=True)
        score_grad = (probs_full * (prob_grad - row_delta)).astype(jnp.bfloat16)
        query_pieces.append(
            jnp.dot(score_grad, keys_all[:, head_index], preferred_element_type=jnp.float32)
            * score_scale
        )
        key_pieces.append(
            jnp.einsum(
                "qk,qe->ke", score_grad, queries[:, head_index], preferred_element_type=jnp.float32
            )
            * score_scale
        )
        value_pieces.append(
            jnp.einsum("qk,qe->ke", probs_low, head_grad, preferred_element_type=jnp.float32)
        )
    own_keys, own_values = (
        lax.psum_scatter(jnp.stack(key_pieces, axis=1), "ctx", scatter_dimension=0, tiled=True),
        lax.psum_scatter(jnp.stack(value_pieces, axis=1), "ctx", scatter_dimension=0, tiled=True),
    )
    query_turned = rotate_back(jnp.stack(query_pieces, axis=1), cosine_table, sine_table)
    key_turned = rotate_back(own_keys, cosine_table, sine_table)
    proj_grad = (
        jnp.stack([query_turned, key_turned, own_values], axis=1)
        .astype(jnp.bfloat16)
        .reshape(row_count, 3, heads_here * HD)
    )
    qkv_bias_grad = jnp.sum(proj_grad.astype(jnp.float32), axis=0)
    qkv_grad = jnp.einsum("td,tce->dce", normed, proj_grad, preferred_element_type=jnp.float32)
    normed_grad = normed_grad + jnp.einsum(
        "tce,dce->td", proj_grad, qkv_full, preferred_element_type=jnp.float32
    )
    full_grad = lax.psum(normed_grad, "tp")
    gain_grad = jnp.sum(full_grad * standard, axis=0)
    shift_grad = jnp.sum(full_grad, axis=0)
    scaled = full_grad * norm_gain
    input_grad = upstream + inverse * (
        scaled
        - jnp.mean(scaled, axis=1, keepdims=True)
        - standard * jnp.mean(scaled * standard, axis=1, keepdims=True)
    )
    bias_sums = lax.psum((qkv_bias_grad, fc1_bias_grad), ("fsdp", "ctx"))
    reduced = (
        lax.psum_scatter(qkv_grad, ("fsdp", "ctx"), scatter_dimension=0, tiled=True),
        lax.psum_scatter(dense_grad, ("fsdp", "ctx"), scatter_dimension=0, tiled=True),
        lax.psum_scatter(fc1_grad, ("fsdp", "ctx"), scatter_dimension=0, tiled=True),
        lax.psum_scatter(fc2_grad, ("fsdp", "ctx"), scatter_dimension=0, tiled=True),
        lax.psum_scatter(gain_grad, ("fsdp", "ctx"), scatter_dimension=0, tiled=True),
        lax.psum_scatter(shift_grad, ("fsdp", "ctx"), scatter_dimension=0, tiled=True),
        lax.psum_scatter(out_bias_grad, ("fsdp", "ctx"), scatter_dimension=0, tiled=True),
    )
    shards = (
        lax.all_gather(reduced[0], "ctx", axis=0, tiled=True),
        lax.all_gather(reduced[1], "ctx", axis=0, tiled=True),
        lax.all_gather(reduced[2], "ctx", axis=0, tiled=True),
        lax.all_gather(reduced[3], "ctx", axis=0, tiled=True),
        lax.all_gather(reduced[4], "ctx", axis=0, tiled=True),
        lax.all_gather(reduced[5], "ctx", axis=0, tiled=True),
        lax.all_gather(reduced[6], "ctx", axis=0, tiled=True),
    )
    return (
        output[None],
        input_grad[None],
        shards[4],
        shards[5],
        shards[0],
        bias_sums[0],
        shards[1],
        shards[6],
        shards[2],
        bias_sums[1],
        shards[3],
        shards[6],
    )


def solution(mesh):
    placed = (
        P("fsdp", "ctx", None),
        P("fsdp", None),
        P("fsdp", None),
        P("fsdp"),
        P("fsdp"),
        P("fsdp", None, "tp"),
        P(None, "tp"),
        P("fsdp", "tp"),
        P("fsdp"),
        P("fsdp", "tp"),
        P("tp"),
        P("fsdp", "tp"),
        P("fsdp"),
        P("fsdp", "ctx", None),
    )
    return jax.shard_map(
        per_device,
        mesh=mesh,
        in_specs=placed,
        out_specs=(
            P("fsdp", "ctx", None),
            P("fsdp", "ctx", None),
            P("fsdp"),
            P("fsdp"),
            P("fsdp", None, "tp"),
            P(None, "tp"),
            P("fsdp", "tp"),
            P("fsdp"),
            P("fsdp", "tp"),
            P("tp"),
            P("fsdp", "tp"),
            P("fsdp"),
        ),
        check_vma=False,
    )
```

profile of v0, /device:TPU:0, one launch (start us, length us, event | category | flops | bytes accessed | tf_op | source)
XLA Modules:
  0.0 1210.0 jit_solution(16124537954326559841)
XLA Ops:
  7.3 2.7 copy.57
  11.0 6.2 all-gather.2
  17.2 5.5 all-gather.1
  24.5 34.9 %all-gather.19.cloned.1.call-done = bf16[2048,3,512]{0,2,1:T(8,128)(2,1)} async-done(((bf16[512,3,512]{0,2,1:T(8,128)(2,1)}), bf16[2048,3,512]{0,2,1:T(8,128)(2,1)}) %all-gather.19.cloned.1.call-update) | async-done | bytes 6291472 | tf_op jit(solution)/shard_map/all_gather | solution.py:84
  59.3 5.9 fusion.46
  69.2 14.3 %all-gather.23.cloned.1.call-done = bf16[2048,512]{1,0:T(8,128)(2,1)} async-done(((bf16[512,512]{1,0:T(8,128)(2,1)}), bf16[2048,512]{1,0:T(8,128)(2,1)}) %all-gather.23.cloned.1.call-update) | async-done | bytes 2097168 | tf_op jit(solution)/shard_map/all_gather | solution.py:85
  83.5 4.3 fusion.58
  87.8 2.1 slice.201
  90.9 16.0 %all-gather.21.cloned.1.call-done = bf16[1024,2,256]{0,2,1:T(8,128)(2,1)} async-done(((bf16[512,2,256]{0,2,1:T(8,128)(2,1)}), bf16[1024,2,256]{0,2,1:T(8,128)(2,1)}) %all-gather.21.cloned.1.call-update) | async-done | bytes 1048592 | tf_op jit(solution)/shard_map/all_gather | solution.py:132
  114.5 15.7 %all-gather.37.cloned.1.call-done = bf16[1024,1,2,256]{0,3,2,1:T(8,128)(2,1)} async-done(((bf16[512,1,2,256]{0,3,2,1:T(8,128)(2,1)}), bf16[1024,1,2,256]{0,3,2,1:T(8,128)(2,1)}) %all-gather.37.cloned.1.call-update) | async-done | bytes 1048592 | tf_op jit(solution)/shard_map/all_gather | solution.py:133
  130.2 2.5 multiply_reduce_fusion.2
  140.1 2.4 convolution_bitcast_fusion.4
  144.2 3.3 convolution_bitcast_fusion.1
  152.3 12.5 %reduce-scatter.9.cloned.1.call-done = f32[512,2,256]{2,0,1:T(8,128)} async-done(((f32[1024,2,256]{2,0,1:T(8,128)}), f32[512,2,256]{2,0,1:T(8,128)}) %reduce-scatter.9.cloned.1.call-update) | async-done | bytes 1048592 | tf_op jit(solution)/shard_map/reduce_scatter | solution.py:215
  164.9 2.1 convert.64
  169.0 2.1 copy.63
  171.0 28.4 %reduce-scatter.7.cloned.1.call-done = f32[512,2,256]{0,2,1:T(8,128)} async-done(((f32[1024,2,256]{0,2,1:T(8,128)}), f32[512,2,256]{0,2,1:T(8,128)}) %reduce-scatter.7.cloned.1.call-update) | async-done | bytes 1048592 | tf_op jit(solution)/shard_map/reduce_scatter | solution.py:214
  203.1 2.1 copy.61
  205.1 2.1 copy.62
  207.2 8.8 fusion.40
  216.7 42.6 %all-gather.25.cloned.1.call-done = bf16[2048,2048]{1,0:T(8,128)(2,1)} async-done(((bf16[512,2048]{1,0:T(8,128)(2,1)}), bf16[2048,2048]{1,0:T(8,128)(2,1)}) %all-gather.25.cloned.1.call-update) | async-done | bytes 8388624 | tf_op jit(solution)/shard_map/all_gather | solution.py:86
  259.3 17.2 %fusion.20 = (bf16[512,2048]{1,0:T(8,128)(2,1)}, f32[512,2048]{1,0:T(8,128)}) fusion(f32[2048]{0:T(1024)S(1)} %convert_element_type.135, bf16[2048,2048]{1,0:T(8,128)(2,1)} %all-gather.25.cloned.1.call-done, bf16[1,512,2048]{2,1,0:T(8,128)(2,1)S(1)} %copy-done, f32[2048]{0:T(1024)S(1)} %bitcast.223, f32[2048]{0:T(1024)S(1)} %bitcast.214, ...), kind=kOutput, calls=%fused_computation.27 | convolution fusion | flops 4370464768 | bytes 16805888 | tf_op jit(solution)/shard_map/dot_general | solution.py:165
  276.5 42.7 %all-gather.27.cloned.1.call-done = bf16[2048,2048]{1,0:T(8,128)(2,1)} async-done(((bf16[512,2048]{1,0:T(8,128)(2,1)}), bf16[2048,2048]{1,0:T(8,128)(2,1)}) %all-gather.27.cloned.1.call-update) | async-done | bytes 8388624 | tf_op jit(solution)/shard_map/all_gather | solution.py:87
  319.2 9.4 convert_reduce_fusion.2
  329.9 8.8 fusion.92
  339.2 12.5 %convolution_bitcast_fusion = f32[2048,2048]{0,1:T(8,128)} fusion(bf16[512,2048]{1,0:T(8,128)(2,1)} %get-tuple-element.96, bf16[1,512,2048]{2,1,0:T(8,128)(2,1)} %param.27), kind=kOutput, calls=%fused_computation | convolution fusion | flops 4294967296 | bytes 20971520 | tf_op jit(solution)/shard_map/td,tf->df/dot_general | solution.py:178
  353.3 10.8 fusion.99
  364.1 9.8 fusion.100
  374.5 6.5 convolution_add_fusion
  381.0 8.7 bitcast_add_fusion
  389.8 79.9 %reduce-scatter.11.cloned.1.call-done = f32[256,3,512]{2,0,1:T(8,128)} async-done(((f32[2048,3,512]{2,0,1:T(8,128)}), f32[256,3,512]{2,0,1:T(8,128)}) %reduce-scatter.11.cloned.1.call-update) | async-done | bytes 1572880 | tf_op jit(solution)/shard_map/reduce_scatter | solution.py:240
  469.7 119.7 %reduce-scatter.15.cloned.1.call-done = f32[256,2048]{1,0:T(8,128)} async-done(((f32[2048,2048]{1,0:T(8,128)}), f32[256,2048]{1,0:T(8,128)}) %reduce-scatter.15.cloned.1.call-update) | async-done | bytes 2097168 | tf_op jit(solution)/shard_map/reduce_scatter | solution.py:242
  589.5 119.4 %reduce-scatter.17.cloned.1.call-done = f32[256,2048]{0,1:T(8,128)} async-done(((f32[2048,2048]{0,1:T(8,128)}), f32[256,2048]{0,1:T(8,128)}) %reduce-scatter.17.cloned.1.call-update) | async-done | bytes 2097168 | tf_op jit(solution)/shard_map/reduce_scatter | solution.py:243
  710.2 5.2 all-gather.4
  715.4 5.2 all-gather.3
  721.9 9.8 all-gather.31.cloned.1.call-done
  731.8 2.5 copy.66
  734.3 291.4 %all-reduce.7.cloned.1.call-done = (f32[512,2048]{1,0:T(8,128)}, f32[512,2048]{1,0:T(8,128)}) async-done(((f32[512,2048]{1,0:T(8,128)}, f32[512,2048]{1,0:T(8,128)}), (f32[512,2048]{1,0:T(8,128)}, f32[512,2048]{1,0:T(8,128)})) %all-reduce.7.cloned.1.call-update) | async-done | bytes 8388624 | tf_op jit(solution)/shard_map/psum | solution.py:172
  1025.7 3.9 fusion.13
  1029.8 6.1 convert_reduce_fusion
  1035.8 28.5 %all-reduce.3 = (f32[2048]{0:T(1024)S(1)}, f32[2048]{0:T(1024)S(1)}, f32[3,512]{1,0:T(4,128)}, f32[2048]{0:T(1024)S(1)}, f32[2048]{0:T(1024)}) all-reduce(f32[2048]{0:T(1024)S(1)} %get-tuple-element.60, f32[2048]{0:T(1024)S(1)} %get-tuple-element.63, ...), channel_id=5, replica_groups=mesh['fsdp'=4,'ctx'=2,'tp'=4] {'fsdp','ctx'}, use_global_device_ids=true, to_apply=%region_21.22.clone | all-reduce | flops 9728 | bytes 77824
  1064.4 4.4 all-gather.7
  1068.9 4.3 all-gather.5
  1073.2 4.2 all-gather.6
  1077.5 54.2 %all-gather.33.cloned.1.call-done = f32[512,2048]{1,0:T(8,128)} async-done(((f32[256,2048]{1,0:T(8,128)}), f32[512,2048]{1,0:T(8,128)}) %all-gather.33.cloned.1.call-update) | async-done | bytes 4194320 | tf_op jit(solution)/shard_map/all_gather | solution.py:251
  1131.6 58.1 %all-gather.35.cloned.1.call-done = f32[512,2048]{0,1:T(8,128)} async-done(((f32[256,2048]{0,1:T(8,128)}), f32[512,2048]{0,1:T(8,128)}) %all-gather.35.cloned.1.call-update) | async-done | bytes 4194320 | tf_op jit(solution)/shard_map/all_gather | solution.py:252
  1189.8 5.3 copy.67
  1196.9 3.9 copy.84
  (191 shorter events, 45.9 us)
Async XLA Ops:
  7.2 3.7 copy-start.32
  7.2 3.8 copy-start.33
  7.2 3.8 copy-start.34
  7.2 15.5 %copy-start.30 = (bf16[3,512]{1,0:T(4,128)(2,1)S(1)}, bf16[3,512]{1,0:T(4,128)(2,1)}, u32[]{:S(2)}) copy-start(bf16[3,512]{1,0:T(4,128)(2,1)} %param.20) | copy-start | bytes 9220
  7.2 15.5 %copy-start.37 = (s32[1,3]{1,0:T(1,128)S(1)}, s32[1,3]{1,0:T(1,128)}, u32[]{:S(2)}) copy-start(s32[1,3]{1,0:T(1,128)} %param.15) | copy-start | bytes 40
  7.2 15.8 %copy-start = (bf16[1,512,2048]{2,1,0:T(8,128)(2,1)S(1)}, bf16[1,512,2048]{2,1,0:T(8,128)(2,1)}, u32[]{:S(2)}) copy-start(bf16[1,512,2048]{2,1,0:T(8,128)(2,1)} %param.14) | copy-start | bytes 6291460
  7.2 52.1 %all-gather.19.cloned.1.call-start = ((), (), s32[]{:S(2)}) async-start(), calls=%async_computation.6 | async-start | bytes 7864320 | tf_op jit(solution)/shard_map/all_gather | solution.py:84
  10.0 73.5 %all-gather.23.cloned.1.call-start = ((), (), s32[]{:S(2)}) async-start(), calls=%async_computation.8 | async-start | bytes 2621440 | tf_op jit(solution)/shard_map/all_gather | solution.py:85
  10.8 96.1 %all-gather.21.cloned.1.call-start = ((), (), s32[]{:S(2)}) async-start(), calls=%async_computation.7 | async-start | bytes 1572864 | tf_op jit(solution)/shard_map/all_gather | solution.py:132
  11.0 12.1 copy-start.26
  17.2 48.0 %copy-start.28 = (f32[4,1,512]{2,1,0:T(1,128)}, f32[4,1,512]{2,1,0:T(1,128)S(1)}, u32[]{:S(2)}) copy-start(f32[4,1,512]{2,1,0:T(1,128)S(1)} %convert_element_type.153) | copy-start | bytes 24580
  23.0 45.6 %copy-start.27 = (s32[512]{0:T(512)}, s32[512]{0:T(512)S(1)}, u32[]{:S(2)}) copy-start(s32[512]{0:T(512)S(1)} %get-tuple-element.65) | copy-start | bytes 6148
  24.5 41.1 %copy-start.21 = (f32[512,32]{0,1:T(8,128)}, f32[512,32]{0,1:T(8,128)S(1)}, u32[]{:S(2)}) copy-start(f32[512,32]{0,1:T(8,128)S(1)} %get-tuple-element.92) | copy-start | bytes 196612
  24.5 41.1 %copy-start.22 = (f32[512,32]{0,1:T(8,128)}, f32[512,32]{0,1:T(8,128)S(1)}, u32[]{:S(2)}) copy-start(f32[512,32]{0,1:T(8,128)S(1)} %get-tuple-element.93) | copy-start | bytes 196612
  67.8 62.4 %all-gather.37.cloned.1.call-start = ((), (), s32[]{:S(2)}) async-start(), calls=%async_computation.21 | async-start | bytes 1572864 | tf_op jit(solution)/shard_map/all_gather | solution.py:133
  68.0 19.8 %copy-start.25 = (s32[1024]{0:T(1024)}, s32[1024]{0:T(1024)S(1)}, u32[]{:S(2)}) copy-start(s32[1024]{0:T(1024)S(1)} %fusion.79) | copy-start | bytes 12292
  90.0 74.9 %reduce-scatter.9.cloned.1.call-start = ((), (), s32[]{:S(2)}) async-start(), calls=%async_computation.12 | async-start | bytes 3145728 | tf_op jit(solution)/shard_map/reduce_scatter | solution.py:215
  106.9 2.4 copy-start.38
  108.8 2.7 copy-start.1
  108.8 2.7 copy-start.13
  114.3 85.2 %reduce-scatter.7.cloned.1.call-start = ((), (), s32[]{:S(2)}) async-start(), calls=%async_computation.11 | async-start | bytes 3145728 | tf_op jit(solution)/shard_map/reduce_scatter | solution.py:214
  130.2 2.5 copy-start.4
  132.8 2.2 copy-start.19
  133.3 2.9 copy-start.10
  138.6 120.8 %all-gather.25.cloned.1.call-start = ((), (), s32[]{:S(2)}) async-start(), calls=%async_computation.9 | async-start | bytes 10485760 | tf_op jit(solution)/shard_map/all_gather | solution.py:86
  139.3 179.9 %all-gather.27.cloned.1.call-start = ((), (), s32[]{:S(2)}) async-start(), calls=%async_computation.10 | async-start | bytes 10485760 | tf_op jit(solution)/shard_map/all_gather | solution.py:87
  140.1 234.2 %reduce-scatter.13.cloned.1.call-start = ((), (), s32[]{:S(2)}) async-start(), calls=%async_computation.15 | async-start | bytes 4718592 | tf_op jit(solution)/shard_map/reduce_scatter | solution.py:241
  140.1 2.4 copy-start.5
  147.5 322.2 %reduce-scatter.11.cloned.1.call-start = ((), (), s32[]{:S(2)}) async-start(), calls=%async_computation.13 | async-start | bytes 14155776 | tf_op jit(solution)/shard_map/reduce_scatter | solution.py:240
  216.0 43.3 %copy-start.29 = (f32[4,1,512]{2,1,0:T(1,128)S(1)}, f32[4,1,512]{2,1,0:T(1,128)}, u32[]{:S(2)}) copy-start(f32[4,1,512]{2,1,0:T(1,128)} %copy-done.28) | copy-start | bytes 24580
  216.0 373.4 %reduce-scatter.15.cloned.1.call-start = ((), (), s32[]{:S(2)}) async-start(), calls=%async_computation.17 | async-start | bytes 18874368 | tf_op jit(solution)/shard_map/reduce_scatter | solution.py:242
  338.7 370.2 %reduce-scatter.17.cloned.1.call-start = ((), (), s32[]{:S(2)}) async-start(), calls=%async_computation.19 | async-start | bytes 18874368 | tf_op jit(solution)/shard_map/reduce_scatter | solution.py:243
  351.8 380.0 %all-gather.31.cloned.1.call-start = ((), (), s32[]{:S(2)}) async-start(), calls=%async_computation.16 | async-start | bytes 1572864 | tf_op jit(solution)/shard_map/all_gather | solution.py:250
  353.3 10.8 copy-start.42
  374.3 6.7 copy-start.14
  374.3 6.7 copy-start.15
  374.3 651.4 %all-reduce.7.cloned.1.call-start = ((), (), s32[]{:S(2)}) async-start(), calls=%async_computation.22 | async-start | bytes 16777216 | tf_op jit(solution)/shard_map/psum | solution.py:172
  374.5 6.5 copy-start.16
  374.5 6.5 copy-start.40
  389.7 319.2 %copy-start.35 = (bf16[512]{0:T(512)(128)(2,1)S(1)}, bf16[512]{0:T(512)(128)(2,1)}, u32[]{:S(2)}) copy-start(bf16[512]{0:T(512)(128)(2,1)} %param.22) | copy-start | bytes 3076
  389.8 319.2 %copy-start.36 = (bf16[512]{0:T(512)(128)(2,1)S(1)}, bf16[512]{0:T(512)(128)(2,1)}, u32[]{:S(2)}) copy-start(bf16[512]{0:T(512)(128)(2,1)} %param.26) | copy-start | bytes 3076
  389.8 319.2 %copy-start.39 = (u32[32]{0:T(128)S(1)}, u32[32]{0:T(128)}, u32[]{:S(2)}) copy-start(u32[32]{0:T(128)} %constant.160) | copy-start | bytes 388
  389.8 687.7 %all-gather.29.cloned.1.call-start = ((), (), s32[]{:S(2)}) async-start(), calls=%async_computation.14 | async-start | bytes 4718592 | tf_op jit(solution)/shard_map/all_gather | solution.py:249
  469.7 661.9 %all-gather.33.cloned.1.call-start = ((), (), s32[]{:S(2)}) async-start(), calls=%async_computation.18 | async-start | bytes 6291456 | tf_op jit(solution)/shard_map/all_gather | solution.py:251
  589.5 600.3 %all-gather.35.cloned.1.call-start = ((), (), s32[]{:S(2)}) async-start(), calls=%async_computation.20 | async-start | bytes 6291456 | tf_op jit(solution)/shard_map/all_gather | solution.py:252
  1025.7 3.9 copy-start.6
  1025.7 4.1 copy-start.8
  1195.1 6.2 copy-start.9
  (12 other events, 15.8 us)
Sparse Core Ops, SparseCore 0:
  10.2 49.1 all-gather.18
  60.9 22.5 all-gather.22
  85.6 21.2 all-gather.20
  108.9 21.2 all-gather.36
  132.9 31.9 reduce-scatter.8
  167.5 31.8 reduce-scatter.6
  201.0 58.2 all-gather.24
  260.9 58.2 all-gather.26
  323.1 51.0 reduce-scatter.12
  377.6 92.0 reduce-scatter.10
  473.2 116.1 reduce-scatter.14
  592.9 115.9 reduce-scatter.16
  710.4 21.2 all-gather.30
  734.8 290.8 all-reduce.6
  1027.0 46.3 all-gather.28
  1074.9 56.7 all-gather.32
  1133.0 56.7 all-gather.34
where the time goes:
time: 1220 us; the launch traced here: 1210 us
  waiting for transfers between devices  942 us (77%)
  matrix products  122 us (10%)
  blocking collectives  63.4 us (5%)
  local copies, waits for them, and re-layouts  37.8 us (3%)
  other arithmetic  27.6 us (2%)
  between operations  15.6 us (1%)
    psum x1, waiting for transfers between devices, per_device(): summed = lax.psum(partial_out, 'tp')  291 us
    reduce_scatter x1, waiting for transfers between devices, per_device(): lax.psum_scatter(fc1_grad, ('fsdp', 'ctx'), scatter_dimension=0, tiled=True)  120 us
    reduce_scatter x1, waiting for transfers between devices, per_device(): lax.psum_scatter(fc2_grad, ('fsdp', 'ctx'), scatter_dimension=0, tiled=True)  119 us
    reduce_scatter x1, waiting for transfers between devices, per_device(): lax.psum_scatter(qkv_grad, ('fsdp', 'ctx'), scatter_dimension=0, tiled=True)  79.9 us
    all_gather x1, waiting for transfers between devices, per_device(): lax.all_gather(reduced[3], 'ctx', axis=0, tiled=True)  58.1 us
    all_gather x1, waiting for transfers between devices, per_device(): lax.all_gather(reduced[2], 'ctx', axis=0, tiled=True)  54.2 us
    all_gather x1, waiting for transfers between devices, per_device(): lax.all_gather(fc2_weight, 'fsdp', axis=0, tiled=True)  42.7 us
    all_gather x1, waiting for transfers between devices, per_device(): lax.all_gather(fc1_weight, 'fsdp', axis=0, tiled=True)  42.6 us
  transfers between devices with their start and end apart: 17, of which 16 were waited for; matrix products, arithmetic and copies ran while one was open for 14% of the time, Pallas kernels for 0%

commit v1 on v0

--- a/solution.py
+++ b/solution.py
@@ -1,3 +1,4 @@
+import functools
 import math
 import jax
 import jax.numpy as jnp
@@ -8,6 +9,20 @@
 ROT = 64
 NORM_EPSILON = 1e-05
 MASK_FLOOR = -1000000000.0
+
+
+def attach_sheets(work_x, chip_axis):
+    devs = lax.axis_size(chip_axis)
+    local_out = lambda a_next: [(h, h ^ a_next) for h in range(devs)]
+    inter = work_x
+    for c in range(devs.bit_length() - 1):
+        odd = local_out(1 << c)
+        last = lax.ppermute(inter, chip_axis, odd)
+        inter = inter + last
+    return inter
+
+
+push_the_goods = functools.partial(attach_sheets, chip_axis="tp")
 
 
 def rotation_tables(position):
@@ -169,7 +184,7 @@
     partial_out = jnp.einsum(
         "te,de->td", attended, dense_full, preferred_element_type=jnp.float32
     ) + jnp.einsum("tf,df->td", hidden, fc2_full, preferred_element_type=jnp.float32)
-    summed = lax.psum(partial_out, "tp")
+    summed = push_the_goods(partial_out)
     output = (inputs + summed + out_bias).astype(jnp.bfloat16)
     upstream_low = cotangent[0]
     upstream = upstream_low.astype(jnp.float32)

time: 1220 us -> 1110 us (0.910)
  waiting for transfers between devices: 942 us -> 844 us
    psum x1, waiting for transfers between devices: 291 us -> 189 us  [per_device(): full_grad = lax.psum(normed_grad, 'tp')]
    reduce_scatter x1, waiting for transfers between devices: 0.33 us -> 22.4 us  [per_device(): lax.psum_scatter(dense_grad, ('fsdp', 'ctx'), scatter_dimension=0, tiled=...]
    reduce_scatter x1, waiting for transfers between devices: 120 us -> 107 us  [per_device(): lax.psum_scatter(fc1_grad, ('fsdp', 'ctx'), scatter_dimension=0, tiled=True)]
    unnamed x103 -> x105, local copies, waits for them, and re-layouts: 26 us -> 24.3 us
  transfers between devices with their start and end apart: 17 -> 19, of which waited for: 16 -> 16; matrix products, arithmetic and copies ran while one was open for 14% -> 14% of each run, Pallas kernels for 0% -> 0%
where the time goes in v1:
time: 1110 us
  waiting for transfers between devices  844 us (76%)
  matrix products  110 us (10%)
  blocking collectives  63.1 us (6%)
  local copies, waits for them, and re-layouts  36.2 us (3%)
  other arithmetic  31.4 us (3%)
  between operations  15.6 us (1%)
    psum x1, waiting for transfers between devices, per_device(): full_grad = lax.psum(normed_grad, 'tp')  189 us
    reduce_scatter x1, waiting for transfers between devices, per_device(): lax.psum_scatter(fc2_grad, ('fsdp', 'ctx'), scatter_dimension=0, tiled=True)  110 us
    reduce_scatter x1, waiting for transfers between devices, per_device(): lax.psum_scatter(fc1_grad, ('fsdp', 'ctx'), scatter_dimension=0, tiled=True)  107 us
    reduce_scatter x1, waiting for transfers between devices, per_device(): lax.psum_scatter(qkv_grad, ('fsdp', 'ctx'), scatter_dimension=0, tiled=True)  78.6 us
    all_gather x1, waiting for transfers between devices, per_device(): lax.all_gather(reduced[3], 'ctx', axis=0, tiled=True)  58.1 us
    all_gather x1, waiting for transfers between devices, per_device(): lax.all_gather(reduced[2], 'ctx', axis=0, tiled=True)  53.5 us
    all_gather x1, waiting for transfers between devices, per_device(): lax.all_gather(fc2_weight, 'fsdp', axis=0, tiled=True)  42.7 us
    all_gather x1, waiting for transfers between devices, per_device(): lax.all_gather(fc1_weight, 'fsdp', axis=0, tiled=True)  42.6 us
  transfers between devices with their start and end apart: 19, of which 16 were waited for; matrix products, arithmetic and copies ran while one was open for 14% of the time, Pallas kernels for 0%

profile of v1, /device:TPU:0, one launch (start us, length us, event | category | flops | bytes accessed | tf_op | source)
XLA Modules:
  0.0 1105.3 jit_solution(8441367324626753058)
XLA Ops:
  7.3 2.7 copy.57
  11.0 6.2 all-gather.2
  17.2 5.5 all-gather.1
  24.5 34.9 %all-gather.19.cloned.1.call-done = bf16[2048,3,512]{0,2,1:T(8,128)(2,1)} async-done(((bf16[512,3,512]{0,2,1:T(8,128)(2,1)}), bf16[2048,3,512]{0,2,1:T(8,128)(2,1)}) %all-gather.19.cloned.1.call-update) | async-done | bytes 6291472 | tf_op jit(solution)/shard_map/all_gather | solution.py:99
  59.3 5.9 fusion.46
  68.0 15.5 %all-gather.23.cloned.1.call-done = bf16[2048,512]{1,0:T(8,128)(2,1)} async-done(((bf16[512,512]{1,0:T(8,128)(2,1)}), bf16[2048,512]{1,0:T(8,128)(2,1)}) %all-gather.23.cloned.1.call-update) | async-done | bytes 2097168 | tf_op jit(solution)/shard_map/all_gather | solution.py:100
  83.5 3.7 fusion.58
  87.2 2.1 slice.201
  89.4 17.5 %all-gather.21.cloned.1.call-done = bf16[1024,2,256]{0,2,1:T(8,128)(2,1)} async-done(((bf16[512,2,256]{0,2,1:T(8,128)(2,1)}), bf16[1024,2,256]{0,2,1:T(8,128)(2,1)}) %all-gather.21.cloned.1.call-update) | async-done | bytes 1048592 | tf_op jit(solution)/shard_map/all_gather | solution.py:147
  113.7 16.5 %all-gather.37.cloned.1.call-done = bf16[1024,1,2,256]{0,3,2,1:T(8,128)(2,1)} async-done(((bf16[512,1,2,256]{0,3,2,1:T(8,128)(2,1)}), bf16[1024,1,2,256]{0,3,2,1:T(8,128)(2,1)}) %all-gather.37.cloned.1.call-update) | async-done | bytes 1048592 | tf_op jit(solution)/shard_map/all_gather | solution.py:148
  130.2 2.5 multiply_reduce_fusion.2
  142.4 3.3 convolution_bitcast_fusion.1
  150.0 14.8 %reduce-scatter.9.cloned.1.call-done = f32[512,2,256]{2,0,1:T(8,128)} async-done(((f32[1024,2,256]{2,0,1:T(8,128)}), f32[512,2,256]{2,0,1:T(8,128)}) %reduce-scatter.9.cloned.1.call-update) | async-done | bytes 1048592 | tf_op jit(solution)/shard_map/reduce_scatter | solution.py:230
  164.8 2.1 convert.64
  166.9 2.2 copy.60
  171.1 28.3 %reduce-scatter.7.cloned.1.call-done = f32[512,2,256]{0,2,1:T(8,128)} async-done(((f32[1024,2,256]{0,2,1:T(8,128)}), f32[512,2,256]{0,2,1:T(8,128)}) %reduce-scatter.7.cloned.1.call-update) | async-done | bytes 1048592 | tf_op jit(solution)/shard_map/reduce_scatter | solution.py:229
  203.0 2.1 copy.61
  207.1 8.8 fusion.40
  216.7 42.6 %all-gather.25.cloned.1.call-done = bf16[2048,2048]{1,0:T(8,128)(2,1)} async-done(((bf16[512,2048]{1,0:T(8,128)(2,1)}), bf16[2048,2048]{1,0:T(8,128)(2,1)}) %all-gather.25.cloned.1.call-update) | async-done | bytes 8388624 | tf_op jit(solution)/shard_map/all_gather | solution.py:101
  259.3 17.2 %fusion.20 = (bf16[512,2048]{1,0:T(8,128)(2,1)}, f32[512,2048]{1,0:T(8,128)}) fusion(f32[2048]{0:T(1024)S(1)} %convert_element_type.135, bf16[2048,2048]{1,0:T(8,128)(2,1)} %all-gather.25.cloned.1.call-done, bf16[1,512,2048]{2,1,0:T(8,128)(2,1)S(1)} %copy-done.4, f32[2048]{0:T(1024)S(1)} %bitcast.223, f32[2048]{0:T(1024)S(1)} %bitcast.214, ...), kind=kOutput, calls=%fused_computation.27 | convolution fusion | flops 4370464768 | bytes 16805888 | tf_op jit(solution)/shard_map/dot_general | solution.py:180
  276.5 42.7 %all-gather.27.cloned.1.call-done = bf16[2048,2048]{1,0:T(8,128)(2,1)} async-done(((bf16[512,2048]{1,0:T(8,128)(2,1)}), bf16[2048,2048]{1,0:T(8,128)(2,1)}) %all-gather.27.cloned.1.call-update) | async-done | bytes 8388624 | tf_op jit(solution)/shard_map/all_gather | solution.py:102
  319.2 9.4 convert_reduce_fusion.2
  329.9 8.8 fusion.92
  339.2 12.5 %convolution_bitcast_fusion = f32[2048,2048]{0,1:T(8,128)} fusion(bf16[512,2048]{1,0:T(8,128)(2,1)} %get-tuple-element.102, bf16[1,512,2048]{2,1,0:T(8,128)(2,1)} %param.27), kind=kOutput, calls=%fused_computation | convolution fusion | flops 4294967296 | bytes 20971520 | tf_op jit(solution)/shard_map/td,tf->df/dot_general | solution.py:193
  351.8 22.4 %reduce-scatter.13.cloned.1.call-done = f32[256,512]{0,1:T(8,128)} async-done(((f32[2048,512]{0,1:T(8,128)}), f32[256,512]{0,1:T(8,128)}) %reduce-scatter.13.cloned.1.call-update) | async-done | bytes 524304 | tf_op jit(solution)/shard_map/reduce_scatter | solution.py:256
  374.3 7.7 fusion.100
  382.1 8.8 bitcast_add_fusion
  391.0 78.6 %reduce-scatter.11.cloned.1.call-done = f32[256,3,512]{2,0,1:T(8,128)} async-done(((f32[2048,3,512]{2,0,1:T(8,128)}), f32[256,3,512]{2,0,1:T(8,128)}) %reduce-scatter.11.cloned.1.call-update) | async-done | bytes 1572880 | tf_op jit(solution)/shard_map/reduce_scatter | solution.py:255
  469.8 7.8 fusion.99
  477.6 3.3 convolution_add_fusion
  482.4 107.0 %reduce-scatter.15.cloned.1.call-done = f32[256,2048]{1,0:T(8,128)} async-done(((f32[2048,2048]{1,0:T(8,128)}), f32[256,2048]{1,0:T(8,128)}) %reduce-scatter.15.cloned.1.call-update) | async-done | bytes 2097168 | tf_op jit(solution)/shard_map/reduce_scatter | solution.py:257
  589.7 6.6 add.207
  596.3 2.4 collective-permute-start.1
  598.8 110.1 %reduce-scatter.17.cloned.1.call-done = f32[256,2048]{0,1:T(8,128)} async-done(((f32[2048,2048]{0,1:T(8,128)}), f32[256,2048]{0,1:T(8,128)}) %reduce-scatter.17.cloned.1.call-update) | async-done | bytes 2097168 | tf_op jit(solution)/shard_map/reduce_scatter | solution.py:258
  710.2 5.2 all-gather.4
  715.4 5.2 all-gather.3
  721.9 9.8 all-gather.31.cloned.1.call-done
  731.7 2.5 copy.66
  734.2 188.9 %all-reduce.6.cloned.1.call-done = f32[512,2048]{1,0:T(8,128)} async-done(((f32[512,2048]{1,0:T(8,128)}), f32[512,2048]{1,0:T(8,128)}) %all-reduce.6.cloned.1.call-update) | async-done | bytes 4194320 | tf_op jit(solution)/shard_map/psum | solution.py:244
  923.1 3.8 fusion.13
  927.2 7.1 convert_reduce_fusion
  934.3 28.2 %all-reduce.3 = (f32[2048]{0:T(1024)S(1)}, f32[2048]{0:T(1024)S(1)}, f32[3,512]{1,0:T(4,128)}, f32[2048]{0:T(1024)S(1)}, f32[2048]{0:T(1024)}) all-reduce(f32[2048]{0:T(1024)S(1)} %get-tuple-element.60, f32[2048]{0:T(1024)S(1)} %get-tuple-element.63, ...), channel_id=5, replica_groups=mesh['fsdp'=4,'ctx'=2,'tp'=4] {'fsdp','ctx'}, use_global_device_ids=true, to_apply=%region_20.21.clone | all-reduce | flops 9728 | bytes 77824
  962.6 4.4 all-gather.7
  967.0 4.2 all-gather.5
  971.3 4.2 all-gather.6
  975.6 53.5 %all-gather.33.cloned.1.call-done = f32[512,2048]{1,0:T(8,128)} async-done(((f32[256,2048]{1,0:T(8,128)}), f32[512,2048]{1,0:T(8,128)}) %all-gather.33.cloned.1.call-update) | async-done | bytes 4194320 | tf_op jit(solution)/shard_map/all_gather | solution.py:266
  1029.1 58.1 %all-gather.35.cloned.1.call-done = f32[512,2048]{0,1:T(8,128)} async-done(((f32[256,2048]{0,1:T(8,128)}), f32[512,2048]{0,1:T(8,128)}) %all-gather.35.cloned.1.call-update) | async-done | bytes 4194320 | tf_op jit(solution)/shard_map/all_gather | solution.py:267
  1087.2 5.3 copy.67
  (198 shorter events, 46.6 us)
Async XLA Ops:
  7.2 3.7 copy-start.35
  7.2 3.8 copy-start.36
  7.2 3.8 copy-start.37
  7.2 15.5 %copy-start.33 = (bf16[3,512]{1,0:T(4,128)(2,1)S(1)}, bf16[3,512]{1,0:T(4,128)(2,1)}, u32[]{:S(2)}) copy-start(bf16[3,512]{1,0:T(4,128)(2,1)} %param.20) | copy-start | bytes 9220
  7.2 15.5 %copy-start.40 = (s32[1,3]{1,0:T(1,128)S(1)}, s32[1,3]{1,0:T(1,128)}, u32[]{:S(2)}) copy-start(s32[1,3]{1,0:T(1,128)} %param.15) | copy-start | bytes 40
  7.2 15.8 %copy-start.3 = (bf16[1,512,2048]{2,1,0:T(8,128)(2,1)S(1)}, bf16[1,512,2048]{2,1,0:T(8,128)(2,1)}, u32[]{:S(2)}) copy-start(bf16[1,512,2048]{2,1,0:T(8,128)(2,1)} %param.14) | copy-start | bytes 6291460
  7.2 52.1 %all-gather.19.cloned.1.call-start = ((), (), s32[]{:S(2)}) async-start(), calls=%async_computation.6 | async-start | bytes 7864320 | tf_op jit(solution)/shard_map/all_gather | solution.py:99
  10.0 73.5 %all-gather.23.cloned.1.call-start = ((), (), s32[]{:S(2)}) async-start(), calls=%async_computation.8 | async-start | bytes 2621440 | tf_op jit(solution)/shard_map/all_gather | solution.py:100
  10.8 96.1 %all-gather.21.cloned.1.call-start = ((), (), s32[]{:S(2)}) async-start(), calls=%async_computation.7 | async-start | bytes 1572864 | tf_op jit(solution)/shard_map/all_gather | solution.py:147
  17.2 48.0 %copy-start.31 = (f32[4,1,512]{2,1,0:T(1,128)}, f32[4,1,512]{2,1,0:T(1,128)S(1)}, u32[]{:S(2)}) copy-start(f32[4,1,512]{2,1,0:T(1,128)S(1)} %convert_element_type.153) | copy-start | bytes 24580
  24.4 41.1 %copy-start.27 = (f32[512,32]{0,1:T(8,128)}, f32[512,32]{0,1:T(8,128)S(1)}, u32[]{:S(2)}) copy-start(f32[512,32]{0,1:T(8,128)S(1)} %get-tuple-element.90) | copy-start | bytes 196612
  24.4 41.1 %copy-start.28 = (f32[512,32]{0,1:T(8,128)}, f32[512,32]{0,1:T(8,128)S(1)}, u32[]{:S(2)}) copy-start(f32[512,32]{0,1:T(8,128)S(1)} %get-tuple-element.91) | copy-start | bytes 196612
  65.3 18.2 %copy-start.6 = (bf16[1,512,2048]{2,1,0:T(8,128)(2,1)S(1)}, bf16[1,512,2048]{2,1,0:T(8,128)(2,1)}, u32[]{:S(2)}) copy-start(bf16[1,512,2048]{2,1,0:T(8,128)(2,1)} %param.27) | copy-start | bytes 6291460
  67.8 62.4 %all-gather.37.cloned.1.call-start = ((), (), s32[]{:S(2)}) async-start(), calls=%async_computation.22 | async-start | bytes 1572864 | tf_op jit(solution)/shard_map/all_gather | solution.py:148
  68.0 73.5 %copy-start.29 = (f32[512]{0:T(512)}, f32[512]{0:T(512)S(1)}, u32[]{:S(2)}) copy-start(f32[512]{0:T(512)S(1)} %get-tuple-element.93) | copy-start | bytes 6148
  89.3 75.5 %reduce-scatter.9.cloned.1.call-start = ((), (), s32[]{:S(2)}) async-start(), calls=%async_computation.12 | async-start | bytes 3145728 | tf_op jit(solution)/shard_map/reduce_scatter | solution.py:230
  113.5 85.9 %reduce-scatter.7.cloned.1.call-start = ((), (), s32[]{:S(2)}) async-start(), calls=%async_computation.11 | async-start | bytes 3145728 | tf_op jit(solution)/shard_map/reduce_scatter | solution.py:229
  130.2 2.5 copy-start.1
  137.6 121.7 %all-gather.25.cloned.1.call-start = ((), (), s32[]{:S(2)}) async-start(), calls=%async_computation.9 | async-start | bytes 10485760 | tf_op jit(solution)/shard_map/all_gather | solution.py:101
  138.3 180.8 %all-gather.27.cloned.1.call-start = ((), (), s32[]{:S(2)}) async-start(), calls=%async_computation.10 | async-start | bytes 10485760 | tf_op jit(solution)/shard_map/all_gather | solution.py:102
  139.1 235.1 %reduce-scatter.13.cloned.1.call-start = ((), (), s32[]{:S(2)}) async-start(), calls=%async_computation.16 | async-start | bytes 4718592 | tf_op jit(solution)/shard_map/reduce_scatter | solution.py:256
  142.4 3.4 copy-start.11
  145.8 323.9 %reduce-scatter.11.cloned.1.call-start = ((), (), s32[]{:S(2)}) async-start(), calls=%async_computation.14 | async-start | bytes 14155776 | tf_op jit(solution)/shard_map/reduce_scatter | solution.py:255
  166.9 40.2 %copy-start.4 = (bf16[1,512,2048]{2,1,0:T(8,128)(2,1)S(1)}, bf16[1,512,2048]{2,1,0:T(8,128)(2,1)}, u32[]{:S(2)}) copy-start(bf16[1,512,2048]{2,1,0:T(8,128)(2,1)} %param.14) | copy-start | bytes 6291460
  216.0 43.3 %copy-start.32 = (f32[4,1,512]{2,1,0:T(1,128)S(1)}, f32[4,1,512]{2,1,0:T(1,128)}, u32[]{:S(2)}) copy-start(f32[4,1,512]{2,1,0:T(1,128)} %copy-done.31) | copy-start | bytes 24580
  216.0 373.4 %reduce-scatter.15.cloned.1.call-start = ((), (), s32[]{:S(2)}) async-start(), calls=%async_computation.18 | async-start | bytes 18874368 | tf_op jit(solution)/shard_map/reduce_scatter | solution.py:257
  338.7 370.1 %reduce-scatter.17.cloned.1.call-start = ((), (), s32[]{:S(2)}) async-start(), calls=%async_computation.20 | async-start | bytes 18874368 | tf_op jit(solution)/shard_map/reduce_scatter | solution.py:258
  351.7 380.0 %all-gather.31.cloned.1.call-start = ((), (), s32[]{:S(2)}) async-start(), calls=%async_computation.17 | async-start | bytes 1572864 | tf_op jit(solution)/shard_map/all_gather | solution.py:265
  374.2 548.9 %all-reduce.6.cloned.1.call-start = ((), (), s32[]{:S(2)}) async-start(), calls=%async_computation.13 | async-start | bytes 8388608 | tf_op jit(solution)/shard_map/psum | solution.py:244
  374.3 7.8 copy-start.17
  374.3 7.8 copy-start.19
  374.3 7.8 copy-start.21
  390.9 78.8 %copy-start.30 = (f32[512]{0:T(512)S(1)}, f32[512]{0:T(512)}, u32[]{:S(2)}) copy-start(f32[512]{0:T(512)} %copy-done.29) | copy-start | bytes 6148
  390.9 584.6 %all-gather.29.cloned.1.call-start = ((), (), s32[]{:S(2)}) async-start(), calls=%async_computation.15 | async-start | bytes 4718592 | tf_op jit(solution)/shard_map/all_gather | solution.py:264
  469.6 559.4 %all-gather.33.cloned.1.call-start = ((), (), s32[]{:S(2)}) async-start(), calls=%async_computation.19 | async-start | bytes 6291456 | tf_op jit(solution)/shard_map/all_gather | solution.py:266
  469.8 7.8 copy-start.24
  481.0 108.8 %collective-permute-start = (f32[512,2048]{1,0:T(8,128)}, f32[512,2048]{1,0:T(8,128)}, u32[]{:S(2)}, u32[]{:S(2)}) collective-permute-start(f32[512,2048]{1,0:T(8,128)} %convolution_add_fusion), channel_id=1, source_target_pairs={{0,1},{1,0},{2,3},{3,2},{4,5},{5,4},{6,7},{7,6},{8,9},{9,8},{10,11... | collective-permute-start | bytes 12582920 | tf_op jit(solution)/shard_map/ppermute | solution.py:20
  589.4 119.4 %copy-start.38 = (bf16[512]{0:T(512)(128)(2,1)S(1)}, bf16[512]{0:T(512)(128)(2,1)}, u32[]{:S(2)}) copy-start(bf16[512]{0:T(512)(128)(2,1)} %param.22) | copy-start | bytes 3076
  589.4 119.5 %copy-start.39 = (bf16[512]{0:T(512)(128)(2,1)S(1)}, bf16[512]{0:T(512)(128)(2,1)}, u32[]{:S(2)}) copy-start(bf16[512]{0:T(512)(128)(2,1)} %param.26) | copy-start | bytes 3076
  589.5 119.5 %copy-start.42 = (u32[32]{0:T(128)S(1)}, u32[32]{0:T(128)}, u32[]{:S(2)}) copy-start(u32[32]{0:T(128)} %constant.160) | copy-start | bytes 388
  589.5 131.1 %copy-start.18 = (bf16[512,1,512]{2,0,1:T(8,128)(2,1)S(1)}, bf16[512,1,512]{2,0,1:T(8,128)(2,1)}, u32[]{:S(2)}) copy-start(bf16[512,1,512]{2,0,1:T(8,128)(2,1)} %copy.63) | copy-start | bytes 1572868
  589.5 131.1 %copy-start.20 = (bf16[512,1,512]{2,0,1:T(8,128)(2,1)S(1)}, bf16[512,1,512]{2,0,1:T(8,128)(2,1)}, u32[]{:S(2)}) copy-start(bf16[512,1,512]{2,0,1:T(8,128)(2,1)} %copy.61) | copy-start | bytes 1572868
  589.5 497.7 %all-gather.35.cloned.1.call-start = ((), (), s32[]{:S(2)}) async-start(), calls=%async_computation.21 | async-start | bytes 6291456 | tf_op jit(solution)/shard_map/all_gather | solution.py:267
  596.3 330.6 %collective-permute-start.1 = (f32[512,2048]{1,0:T(8,128)}, f32[512,2048]{1,0:T(8,128)}, u32[]{:S(2)}, u32[]{:S(2)}) collective-permute-start(f32[512,2048]{1,0:T(8,128)} %add.207), channel_id=1, source_target_pairs={{0,2},{1,3},{2,0},{3,1},{4,6},{5,7},{6,4},{7,5},{8,10},{9,11},{10,... | collective-permute-start | bytes 12582920 | tf_op jit(solution)/shard_map/ppermute | solution.py:20
  923.1 3.8 copy-start.5
  923.1 4.1 copy-start.8
  975.6 118.7 %copy-start.14 = (f32[512,3,512]{2,0,1:T(8,128)S(1)}, f32[512,3,512]{2,0,1:T(8,128)}, u32[]{:S(2)}) copy-start(f32[512,3,512]{2,0,1:T(8,128)} %all-gather.29.cloned.1.call-done) | copy-start | bytes 9437188
  1092.6 4.0 copy-start.9
  (15 other events, 22.3 us)
Sparse Core Ops, SparseCore 0:
  10.2 49.1 all-gather.18
  60.9 22.5 all-gather.22
  85.6 21.2 all-gather.20
  108.9 21.2 all-gather.36
  132.9 31.8 reduce-scatter.8
  167.5 31.8 reduce-scatter.6
  201.0 58.2 all-gather.24
  260.9 58.2 all-gather.26
  323.1 51.0 reduce-scatter.12
  377.5 92.0 reduce-scatter.10
  473.2 116.1 reduce-scatter.14
  592.8 115.9 reduce-scatter.16
  710.4 21.2 all-gather.30
  734.5 188.5 all-reduce.5
  924.5 46.3 all-gather.28
  972.3 56.7 all-gather.32
  1030.5 56.7 all-gather.34
